TPU v7x, 32 devices: a whole 2x2x4 slice. The times are simulated.
32 devices in a mesh: row: 8 (over z, core), col: 4 (over y, x).
Axes of the slice: x: 2, y: 2, z: 4, core: 2. Of those that a mesh axis runs over, the one named last changes fastest.
Arguments:
- rhs: bfloat16 [3, 8, 64, 256], P(None, 'row'), may hold values from -6 to 6
- dinv: bfloat16 [3, 8, 256, 256], P(None, 'row'), as said below
- tiles: bfloat16 [2, 8, 8, 256, 256], P(None, 'row', 'col'), may hold values from -0.09375 to 0.09375
- pattern: int32 [2, 2, 8, 8], P(None, None, 'row', 'col'), may hold values from 0 to 7, as said below
Outputs:
- solution: float32 [3, 8, 64, 256], P(None, 'row')
Inputs may be any that keep to these rules, and one draw needn't show every extreme that they name: pattern[0, l, p, t] = p; pattern[1, l, p, t] = j has (j) modulo the size of col equal to t // 2; positions may repeat, and repeated tiles add. `dinv`: lower triangular with a positive diagonal.
All inputs are finite; a program needn't handle non-finite values.
Results may differ from a plain program's by a relative error of at most 0.0055.
Values may be sent and summed in bfloat16 or wider, within the bound.
No kernel may reach another device: no remote copies, remote signals or barrier semaphores. Data moves between devices by JAX's collectives and lax.ppermute only.
A program may use at most 64 MiB of HBM per device.

v0:
```python
import jax
import jax.numpy as jnp
from jax import lax
from jax.sharding import PartitionSpec as P


def broadcast(block, axis, holder):
    block = jnp.where(lax.axis_index(axis) == holder, block, jnp.zeros_like(block))
    return lax.psum(block, axis)


def collect(rounded, mine_col, col_count, repeat):
    whole_level = lax.all_gather(rounded, "row", axis=0, tiled=True)
    shaped = whole_level.reshape((repeat, col_count) + rounded.shape)
    picked = lax.dynamic_index_in_dim(shaped, mine_col, 1, keepdims=False)
    return picked.reshape((-1,) + rounded.shape[1:])


def per_device(rhs, dinv, tiles, pattern):
    blocks = rhs.shape[1]
    levels_all = rhs.shape[0]
    col_count = lax.axis_size("col")
    row_count = lax.axis_size("row")
    repeat = row_count // col_count
    mine_row = lax.axis_index("row")
    mine_col = lax.axis_index("col")
    targets = pattern[0, :, 0, :] % blocks
    raw_cols = pattern[1, :, 0, :]
    sources = raw_cols // blocks // col_count * blocks + raw_cols % blocks
    row_pick = (targets[:, None, :] == jnp.arange(blocks, dtype=jnp.int32)[None, :, None]).astype(
        jnp.float32
    )
    col_pick = (
        sources[:, None, :] == jnp.arange(repeat * blocks, dtype=jnp.int32)[None, :, None]
    ).astype(jnp.float32)
    fronts = [rhs]
    forward_all = [[] for front in fronts]
    rounded_all = [None for front in fronts]
    for level_now in range(levels_all):
        front_index = 0
        front_level = fronts[front_index][level_now]
        current = front_level.astype(jnp.float32)
        if level_now > 0:
            nearby = collect(rounded_all[front_index], mine_col, col_count, repeat)
            source = jnp.take(nearby, sources[level_now - 1], axis=0)
            product = jnp.einsum(
                "sjb,sab->sja", source, tiles[level_now - 1, 0], preferred_element_type=jnp.float32
            )
            partial_value = jnp.sum(
                row_pick[level_now - 1][:, :, None, None] * product[None], axis=1
            )
            total_sum = lax.psum(partial_value, "col")
            current = current - total_sum
        solved = jnp.einsum(
            "rjb,rab->rja",
            current.astype(jnp.bfloat16),
            dinv[level_now],
            preferred_element_type=jnp.float32,
        )
        forward_all[front_index].append(solved)
        rounded_all[front_index] = solved.astype(jnp.bfloat16)
    backward_all = [[None] * levels_all for front in fronts]
    following_all = [None for front in fronts]
    for level_now in range(levels_all - 1, -1, -1):
        front_index = 0
        remainder = forward_all[front_index][level_now]
        if level_now < levels_all - 1:
            source = jnp.take(following_all[front_index], targets[level_now], axis=0)
            product = jnp.einsum(
                "sja,sab->sjb", source, tiles[level_now, 0], preferred_element_type=jnp.float32
            )
            partial_value = jnp.sum(col_pick[level_now][:, :, None, None] * product[None], axis=1)
            column_total = lax.psum(partial_value, "row")
            shaped = column_total.reshape((repeat, blocks) + column_total.shape[1:])
            picked = lax.dynamic_index_in_dim(shaped, mine_row // col_count, 0, keepdims=False)
            arrived = broadcast(picked, "col", mine_row % col_count)
            remainder = remainder - arrived
        solved = jnp.einsum(
            "rjb,rba->rja",
            remainder.astype(jnp.bfloat16),
            dinv[level_now],
            preferred_element_type=jnp.float32,
        )
        backward_all[front_index][level_now] = solved
        following_all[front_index] = solved.astype(jnp.bfloat16)
    front_index = 0
    levels_stack = jnp.stack(backward_all[front_index])
    return levels_stack


def solution(mesh):
    in_specs = (
        P(None, "row", None, None),
        P(None, "row", None, None),
        P(None, "row", "col", None, None),
        P(None, None, "row", "col"),
    )
    out_specs = P(None, "row", None, None)
    return jax.shard_map(
        per_device, mesh=mesh, in_specs=in_specs, out_specs=out_specs, check_vma=False
    )
```

profile of v0, /device:TPU:0, one launch (start us, length us, event | category | flops | bytes accessed | tf_op | source)
XLA Modules:
  0.0 337.1 jit_solution(15482950410898514648)
XLA Ops:
  6.5 1.1 fusion.57
  7.7 15.9 %all-gather = bf16[512,256]{1,0:T(8,128)(2,1)S(1)} all-gather(bf16[64,256]{1,0:T(8,128)(2,1)S(1)} %get-tuple-element.15), channel_id=2, replica_groups=mesh['row'=8,'col'=4] {'row'}, dimensions={0}, use_global_device_ids=true | all-gather | bytes 294912 | tf_op jit(solution)/shard_map/all_gather | solution.py:13
  23.7 0.6 gather_fusion
  24.3 0.8 convolution_bitcast_fusion.2
  25.2 43.0 %all-reduce.7.cloned.1.call-done = f32[1,64,256]{2,1,0:T(8,128)} async-done(((f32[1,64,256]{2,1,0:T(8,128)}), f32[1,64,256]{2,1,0:T(8,128)}) %all-reduce.7.cloned.1.call-update) | async-done | bytes 65552 | tf_op jit(solution)/shard_map/psum | solution.py:52
  68.2 1.0 fusion.58
  69.2 14.3 %all-gather.1 = bf16[512,256]{1,0:T(8,128)(2,1)S(1)} all-gather(bf16[64,256]{1,0:T(8,128)(2,1)S(1)} %get-tuple-element.17), channel_id=3, replica_groups=mesh['row'=8,'col'=4] {'row'}, dimensions={0}, use_global_device_ids=true | all-gather | bytes 294912 | tf_op jit(solution)/shard_map/all_gather | solution.py:13
  83.5 0.5 gather_fusion.1
  84.0 0.8 convolution_bitcast_fusion.1
  84.9 41.9 %all-reduce.9.cloned.1.call-done = f32[1,64,256]{2,1,0:T(8,128)} async-done(((f32[1,64,256]{2,1,0:T(8,128)}), f32[1,64,256]{2,1,0:T(8,128)}) %all-reduce.9.cloned.1.call-update) | async-done | bytes 65552 | tf_op jit(solution)/shard_map/psum | solution.py:52
  126.9 1.1 fusion.59
  128.0 0.2 fusion.1
  128.2 0.8 multiply_reduce_fusion.1
  129.0 55.1 %all-reduce.11.cloned.1.call-done = f32[2,64,256]{2,1,0:T(8,128)} async-done(((f32[2,64,256]{2,1,0:T(8,128)}), f32[2,64,256]{2,1,0:T(8,128)}) %all-reduce.11.cloned.1.call-update) | async-done | bytes 131088 | tf_op jit(solution)/shard_map/psum | solution.py:73
  184.1 1.5 dynamic-slice_select_fusion.1
  185.7 42.1 %all-reduce.13.cloned.1.call-done = f32[1,64,256]{2,1,0:T(8,128)} async-done(((f32[1,64,256]{2,1,0:T(8,128)}), f32[1,64,256]{2,1,0:T(8,128)}) %all-reduce.13.cloned.1.call-update) | async-done | bytes 65552 | tf_op jit(solution)/shard_map/psum | solution.py:9
  227.8 1.0 fusion.64
  228.8 0.2 fusion.4
  228.9 0.7 multiply_reduce_fusion
  229.8 55.1 %all-reduce.15.cloned.1.call-done = f32[2,64,256]{2,1,0:T(8,128)} async-done(((f32[2,64,256]{2,1,0:T(8,128)}), f32[2,64,256]{2,1,0:T(8,128)}) %all-reduce.15.cloned.1.call-update) | async-done | bytes 131088 | tf_op jit(solution)/shard_map/psum | solution.py:73
  284.9 1.5 dynamic-slice_select_fusion
  286.4 42.2 %all-reduce.17.cloned.1.call-done = f32[1,64,256]{2,1,0:T(8,128)} async-done(((f32[1,64,256]{2,1,0:T(8,128)}), f32[1,64,256]{2,1,0:T(8,128)}) %all-reduce.17.cloned.1.call-update) | async-done | bytes 65552 | tf_op jit(solution)/shard_map/psum | solution.py:9
  328.5 1.0 convolution_bitcast_fusion
  329.5 0.7 pad_maximum_fusion
  (28 shorter events, 0.4 us)
Async XLA Ops:
  6.5 17.7 %copy-start.1 = (bf16[2,1,2,256,256]{4,3,2,1,0:T(8,128)(2,1)S(1)}, bf16[2,1,2,256,256]{4,3,2,1,0:T(8,128)(2,1)}, u32[]{:S(2)}) copy-start(bf16[2,1,2,256,256]{4,3,2,1,0:T(8,128)(2,1)} %param.10) | copy-start | bytes 1572868
  6.5 61.6 %all-reduce.7.cloned.1.call-start = ((), (), s32[]{:S(2)}) async-start(), calls=%async_computation | async-start | bytes 131072 | tf_op jit(solution)/shard_map/psum | solution.py:52
  7.7 16.0 %slice-start = ((s32[2,2,1,2]{3,2,1,0:T(1,128)}), s32[1,2,1,2]{3,2,1,0:T(1,128)S(1)}, s32[]{:S(2)}) async-start(s32[2,2,1,2]{3,2,1,0:T(1,128)} %param.11), calls=%async_computation.6 | async-start | bytes 2048 | tf_op jit(solution)/shard_map/slice | solution.py:28
  23.6 44.5 %copy-start = (bf16[3,1,256,256]{3,2,1,0:T(8,128)(2,1)S(1)}, bf16[3,1,256,256]{3,2,1,0:T(8,128)(2,1)}, u32[]{:S(2)}) copy-start(bf16[3,1,256,256]{3,2,1,0:T(8,128)(2,1)} %param.9) | copy-start | bytes 1179652
  24.3 43.9 %copy-start.2 = (bf16[3,1,64,256]{3,2,1,0:T(8,128)(2,1)S(1)}, bf16[3,1,64,256]{3,2,1,0:T(8,128)(2,1)}, u32[]{:S(2)}) copy-start(bf16[3,1,64,256]{3,2,1,0:T(8,128)(2,1)} %param.8) | copy-start | bytes 294916
  25.1 101.7 %all-reduce.9.cloned.1.call-start = ((), (), s32[]{:S(2)}) async-start(), calls=%async_computation.1 | async-start | bytes 131072 | tf_op jit(solution)/shard_map/psum | solution.py:52
  84.9 99.2 %all-reduce.11.cloned.1.call-start = ((), (), s32[]{:S(2)}) async-start(), calls=%async_computation.2 | async-start | bytes 262144 | tf_op jit(solution)/shard_map/psum | solution.py:73
  128.9 98.8 %all-reduce.13.cloned.1.call-start = ((), (), s32[]{:S(2)}) async-start(), calls=%async_computation.3 | async-start | bytes 131072 | tf_op jit(solution)/shard_map/psum | solution.py:9
  185.6 99.3 %all-reduce.15.cloned.1.call-start = ((), (), s32[]{:S(2)}) async-start(), calls=%async_computation.4 | async-start | bytes 262144 | tf_op jit(solution)/shard_map/psum | solution.py:73
  229.7 98.8 %all-reduce.17.cloned.1.call-start = ((), (), s32[]{:S(2)}) async-start(), calls=%async_computation.5 | async-start | bytes 131072 | tf_op jit(solution)/shard_map/psum | solution.py:9
Sparse Core Ops, SparseCore 0:
  25.3 42.8 all-reduce.6
  85.0 41.7 all-reduce.8
  129.2 54.9 all-reduce.10
  186.8 40.8 all-reduce.12
  229.9 54.9 all-reduce.14
  287.6 40.8 all-reduce.16
where the time goes:
time: 337 us
  waiting for transfers between devices  279 us (83%)
  blocking collectives  30.2 us (9%)
  between operations  13.6 us (4%)
  matrix products  7.25 us (2%)
  other arithmetic  5.19 us (2%)
    psum x2, waiting for transfers between devices, per_device(): column_total = lax.psum(partial_value, 'row')  110 us
    psum x2, waiting for transfers between devices, per_device(): total_sum = lax.psum(partial_value, 'col')  84.9 us
    psum x2, waiting for transfers between devices, broadcast(): return lax.psum(block, axis)  84.3 us
    all_gather x2, blocking collectives, collect(): whole_level = lax.all_gather(rounded, 'row', axis=0, tiled=True)  30.2 us
  transfers between devices with their start and end apart: 6, of which 6 were waited for; matrix products, arithmetic and copies ran while one was open for 0% of the time, Pallas kernels for 0%

commit v1 on v0

--- a/solution.py
+++ b/solution.py
@@ -70,7 +70,11 @@
                 "sja,sab->sjb", source, tiles[level_now, 0], preferred_element_type=jnp.float32
             )
             partial_value = jnp.sum(col_pick[level_now][:, :, None, None] * product[None], axis=1)
-            column_total = lax.psum(partial_value, "row")
+            column_total = partial_value
+            for hop in (1, 2, 4):
+                column_total = column_total + lax.ppermute(
+                    column_total, "row", [(dev, dev ^ hop) for dev in range(8)]
+                )
             shaped = column_total.reshape((repeat, blocks) + column_total.shape[1:])
             picked = lax.dynamic_index_in_dim(shaped, mine_row // col_count, 0, keepdims=False)
             arrived = broadcast(picked, "col", mine_row % col_count)

time: 337 us -> 255 us (0.76)
  waiting for transfers between devices: 279 us -> 192 us
  starting transfers between devices: 0.21 us -> 8.32 us
    psum x2 -> x0, waiting for transfers between devices: 110 us -> none  [per_device(): column_total = lax.psum(partial_value, 'row')]
    ppermute x0 -> x6, waiting for transfers between devices: none -> 22.8 us  [per_device(): lax.ppermute(column_total, 'row', [(dev, dev ^ hop) for dev in range(8)])]
    ppermute x0 -> x6, starting transfers between devices: none -> 8.19 us  [per_device(): lax.ppermute(column_total, 'row', [(dev, dev ^ hop) for dev in range(8)])]
  transfers between devices with their start and end apart: 6 -> 10, of which waited for: 6 -> 10; matrix products, arithmetic and copies ran while one was open for 0% -> 0% of each run, Pallas kernels for 0% -> 0%
where the time goes in v1:
time: 255 us
  waiting for transfers between devices  192 us (75%)
  blocking collectives  30.2 us (12%)
  between operations  13.3 us (5%)
  starting transfers between devices  8.32 us (3%)
  matrix products  7.2 us (3%)
    psum x2, waiting for transfers between devices, per_device(): total_sum = lax.psum(partial_value, 'col')  84.9 us
    psum x2, waiting for transfers between devices, broadcast(): return lax.psum(block, axis)  83.9 us
    all_gather x2, blocking collectives, collect(): whole_level = lax.all_gather(rounded, 'row', axis=0, tiled=True)  30.2 us
    ppermute x6, waiting for transfers between devices, per_device(): lax.ppermute(column_total, 'row', [(dev, dev ^ hop) for dev in range(8)])  22.8 us
    ppermute x6, starting transfers between devices, per_device(): lax.ppermute(column_total, 'row', [(dev, dev ^ hop) for dev in range(8)])  8.19 us
  transfers between devices with their start and end apart: 10, of which 10 were waited for; matrix products, arithmetic and copies ran while one was open for 0% of the time, Pallas kernels for 0%

profile of v1, /device:TPU:0, one launch (start us, length us, event | category | flops | bytes accessed | tf_op | source)
XLA Modules:
  0.0 254.7 jit_solution(6252298760742957231)
XLA Ops:
  6.5 0.7 slice.51
  7.3 1.1 fusion.59
  8.4 15.9 %all-gather = bf16[512,256]{1,0:T(8,128)(2,1)S(1)} all-gather(bf16[64,256]{1,0:T(8,128)(2,1)S(1)} %get-tuple-element.15), channel_id=2, replica_groups=mesh['row'=8,'col'=4] {'row'}, dimensions={0}, use_global_device_ids=true | all-gather | bytes 294912 | tf_op jit(solution)/shard_map/all_gather | solution.py:13
  24.9 0.8 convolution_bitcast_fusion.2
  25.9 42.9 %all-reduce.5.cloned.1.call-done = f32[1,64,256]{2,1,0:T(8,128)} async-done(((f32[1,64,256]{2,1,0:T(8,128)}), f32[1,64,256]{2,1,0:T(8,128)}) %all-reduce.5.cloned.1.call-update) | async-done | bytes 65552 | tf_op jit(solution)/shard_map/psum | solution.py:52
  68.8 1.0 fusion.60
  69.8 14.3 %all-gather.1 = bf16[512,256]{1,0:T(8,128)(2,1)S(1)} all-gather(bf16[64,256]{1,0:T(8,128)(2,1)S(1)} %get-tuple-element.17), channel_id=3, replica_groups=mesh['row'=8,'col'=4] {'row'}, dimensions={0}, use_global_device_ids=true | all-gather | bytes 294912 | tf_op jit(solution)/shard_map/all_gather | solution.py:13
  84.7 0.8 convolution_bitcast_fusion.1
  85.6 41.9 %all-reduce.7.cloned.1.call-done = f32[1,64,256]{2,1,0:T(8,128)} async-done(((f32[1,64,256]{2,1,0:T(8,128)}), f32[1,64,256]{2,1,0:T(8,128)}) %all-reduce.7.cloned.1.call-update) | async-done | bytes 65552 | tf_op jit(solution)/shard_map/psum | solution.py:52
  127.5 1.1 fusion.61
  129.0 1.3 collective-permute-done
  130.3 1.6 collective-permute-start.1
  131.9 4.1 %collective-permute-done.1 = f32[2,64,256]{2,1,0:T(8,128)S(1)} collective-permute-done((f32[2,64,256]{2,1,0:T(8,128)S(1)}, f32[2,64,256]{2,1,0:T(8,128)S(1)}, u32[]{:S(2)}, u32[]{:S(2)}) %collective-permute-start.1) | collective-permute-done | bytes 131104 | tf_op jit(solution)/shard_map/ppermute | solution.py:75
  136.0 2.5 collective-permute-start.2
  138.5 6.0 %collective-permute-done.2 = f32[2,64,256]{2,1,0:T(8,128)S(1)} collective-permute-done((f32[2,64,256]{2,1,0:T(8,128)S(1)}, f32[2,64,256]{2,1,0:T(8,128)S(1)}, u32[]{:S(2)}, u32[]{:S(2)}) %collective-permute-start.2) | collective-permute-done | bytes 131104 | tf_op jit(solution)/shard_map/ppermute | solution.py:75
  145.2 41.9 %all-reduce.9.cloned.1.call-done = f32[1,64,256]{2,1,0:T(8,128)} async-done(((f32[1,64,256]{2,1,0:T(8,128)}), f32[1,64,256]{2,1,0:T(8,128)}) %all-reduce.9.cloned.1.call-update) | async-done | bytes 65552 | tf_op jit(solution)/shard_map/psum | solution.py:9
  187.1 1.0 fusion.66
  188.4 1.3 collective-permute-done.3
  189.8 1.6 collective-permute-start.4
  191.3 4.1 %collective-permute-done.4 = f32[2,64,256]{2,1,0:T(8,128)S(1)} collective-permute-done((f32[2,64,256]{2,1,0:T(8,128)S(1)}, f32[2,64,256]{2,1,0:T(8,128)S(1)}, u32[]{:S(2)}, u32[]{:S(2)}) %collective-permute-start.4) | collective-permute-done | bytes 131104 | tf_op jit(solution)/shard_map/ppermute | solution.py:75
  195.4 2.5 collective-permute-start.5
  197.9 6.0 %collective-permute-done.5 = f32[2,64,256]{2,1,0:T(8,128)S(1)} collective-permute-done((f32[2,64,256]{2,1,0:T(8,128)S(1)}, f32[2,64,256]{2,1,0:T(8,128)S(1)}, u32[]{:S(2)}, u32[]{:S(2)}) %collective-permute-start.5) | collective-permute-done | bytes 131104 | tf_op jit(solution)/shard_map/ppermute | solution.py:75
  204.5 42.0 %all-reduce.11.cloned.1.call-done = f32[1,64,256]{2,1,0:T(8,128)} async-done(((f32[1,64,256]{2,1,0:T(8,128)}), f32[1,64,256]{2,1,0:T(8,128)}) %all-reduce.11.cloned.1.call-update) | async-done | bytes 65552 | tf_op jit(solution)/shard_map/psum | solution.py:9
  246.5 1.0 convolution_bitcast_fusion
  (37 shorter events, 4.1 us)
Async XLA Ops:
  6.5 18.4 %copy-start.1 = (bf16[2,1,2,256,256]{4,3,2,1,0:T(8,128)(2,1)S(1)}, bf16[2,1,2,256,256]{4,3,2,1,0:T(8,128)(2,1)}, u32[]{:S(2)}) copy-start(bf16[2,1,2,256,256]{4,3,2,1,0:T(8,128)(2,1)} %param.10) | copy-start | bytes 1572868
  6.5 62.3 %all-reduce.5.cloned.1.call-start = ((), (), s32[]{:S(2)}) async-start(), calls=%async_computation | async-start | bytes 131072 | tf_op jit(solution)/shard_map/psum | solution.py:52
  24.3 44.5 %copy-start = (bf16[3,1,256,256]{3,2,1,0:T(8,128)(2,1)S(1)}, bf16[3,1,256,256]{3,2,1,0:T(8,128)(2,1)}, u32[]{:S(2)}) copy-start(bf16[3,1,256,256]{3,2,1,0:T(8,128)(2,1)} %param.9) | copy-start | bytes 1179652
  24.9 43.9 %copy-start.2 = (bf16[3,1,64,256]{3,2,1,0:T(8,128)(2,1)S(1)}, bf16[3,1,64,256]{3,2,1,0:T(8,128)(2,1)}, u32[]{:S(2)}) copy-start(bf16[3,1,64,256]{3,2,1,0:T(8,128)(2,1)} %param.8) | copy-start | bytes 294916
  25.8 101.7 %all-reduce.7.cloned.1.call-start = ((), (), s32[]{:S(2)}) async-start(), calls=%async_computation.1 | async-start | bytes 131072 | tf_op jit(solution)/shard_map/psum | solution.py:52
  85.5 101.5 %all-reduce.9.cloned.1.call-start = ((), (), s32[]{:S(2)}) async-start(), calls=%async_computation.2 | async-start | bytes 131072 | tf_op jit(solution)/shard_map/psum | solution.py:9
  128.9 1.4 collective-permute-start
  130.3 5.6 %collective-permute-start.1 = (f32[2,64,256]{2,1,0:T(8,128)S(1)}, f32[2,64,256]{2,1,0:T(8,128)S(1)}, u32[]{:S(2)}, u32[]{:S(2)}) collective-permute-start(f32[2,64,256]{2,1,0:T(8,128)S(1)} %add.70), channel_id=1, source_target_pairs={{0,8},{4,12},{8,0},{12,4},{16,24},{20,28},{24,16},{28,20},{1,9},{5... | collective-permute-start | bytes 393224 | tf_op jit(solution)/shard_map/ppermute | solution.py:75
  136.0 8.5 %collective-permute-start.2 = (f32[2,64,256]{2,1,0:T(8,128)S(1)}, f32[2,64,256]{2,1,0:T(8,128)S(1)}, u32[]{:S(2)}, u32[]{:S(2)}) collective-permute-start(f32[2,64,256]{2,1,0:T(8,128)S(1)} %add.71), channel_id=1, source_target_pairs={{0,16},{4,20},{8,24},{12,28},{16,0},{20,4},{24,8},{28,12},{1,17},{... | collective-permute-start | bytes 393224 | tf_op jit(solution)/shard_map/ppermute | solution.py:75
  145.1 101.4 %all-reduce.11.cloned.1.call-start = ((), (), s32[]{:S(2)}) async-start(), calls=%async_computation.3 | async-start | bytes 131072 | tf_op jit(solution)/shard_map/psum | solution.py:9
  188.3 1.4 collective-permute-start.3
  189.8 5.6 %collective-permute-start.4 = (f32[2,64,256]{2,1,0:T(8,128)S(1)}, f32[2,64,256]{2,1,0:T(8,128)S(1)}, u32[]{:S(2)}, u32[]{:S(2)}) collective-permute-start(f32[2,64,256]{2,1,0:T(8,128)S(1)} %add.74), channel_id=1, source_target_pairs={{0,8},{4,12},{8,0},{12,4},{16,24},{20,28},{24,16},{28,20},{1,9},{5... | collective-permute-start | bytes 393224 | tf_op jit(solution)/shard_map/ppermute | solution.py:75
  195.4 8.5 %collective-permute-start.5 = (f32[2,64,256]{2,1,0:T(8,128)S(1)}, f32[2,64,256]{2,1,0:T(8,128)S(1)}, u32[]{:S(2)}, u32[]{:S(2)}) collective-permute-start(f32[2,64,256]{2,1,0:T(8,128)S(1)} %add.75), channel_id=1, source_target_pairs={{0,16},{4,20},{8,24},{12,28},{16,0},{20,4},{24,8},{28,12},{1,17},{... | collective-permute-start | bytes 393224 | tf_op jit(solution)/shard_map/ppermute | solution.py:75
Sparse Core Ops, SparseCore 0:
  25.9 42.8 all-reduce.4
  85.6 41.7 all-reduce.6
  145.2 41.7 all-reduce.8
  204.6 41.8 all-reduce.10
